TPU v7x, 128 devices: a whole 4x4x4 slice. The times are simulated.
128 devices in a mesh: row: 16 (over y, z_hi, core), col: 8 (over x, z_lo).
Axes of the slice: x: 4, y: 4, z: 4 (z_hi: 2, z_lo: 2; z = z_hi * 2 + z_lo), core: 2. Of those that a mesh axis runs over, the one named last changes fastest.
Arguments:
- prior_voltage: float32 [4, 2048, 4096], P(None, 'row', 'col'), may hold values from 0.5 to 1.5
- baseline_admittance: float32 [4, 2048, 4096], P(None, 'row', 'col'), may hold values from 0.5 to 2
- block_warmth: float32 [4, 512, 1024], P(None, 'row', 'col'), may hold values from 0 to 2
- interlayer_indicator: int32 [3, 2048, 4096], P(None, 'row', 'col'), may hold values 0 or 1
- feeder_indicator: int32 [4, 2048, 4096], P(None, 'row', 'col'), may hold values 0 or 1
- injected_amperes: float32 [4, 2048, 4096], P(None, 'row', 'col'), may hold values from 0.5 to 4
Outputs:
- revised_voltage: float32 [4, 2048, 4096], P(None, 'row', 'col')
- revised_warmth: float32 [4, 512, 1024], P(None, 'row', 'col')
All inputs are finite; a program needn't handle non-finite values. No bound on the sum of `interlayer_indicator` or of `feeder_indicator` on one device may be relied on, other than what follows from the above.
Results may differ from a plain program's by a relative error of at most 0.00002.
Values sent between devices are 32-bit elements; how exact they have to be, the bound alone decides.
A program may use at most 128 MiB of HBM per device.

v0:
```python
import functools

import jax
import jax.numpy as jnp
from jax import lax
from jax.experimental import pallas as pl
from jax.experimental.pallas import tpu as pltpu
from jax.sharding import PartitionSpec as P

F32 = jnp.float32
BF16 = jnp.bfloat16
MESH = pl.DeviceIdType.MESH

LEAK = 0.2
HALF = 0.95
SIGMA = 1.0 / HALF
RHO0 = 1.0 / SIGMA
RHO1 = 1.0 / (2.0 * SIGMA - RHO0)
RHO2 = 1.0 / (2.0 * SIGMA - RHO1)
STEP_1 = (RHO1 * RHO0, 2.0 * RHO1 / HALF)
STEP_2 = (RHO2 * RHO1, 2.0 * RHO2 / HALF)
HEAT_SWEEPS = 4
DT = 0.12
GAIN = 0.0625
MAIN_UNROLL = 4
STRIP_UNROLL = 3

ROWS = 128
M0 = 8
S0 = 144
R_ALL = 176
Q0 = 16
Q_ALL = 160

DIRS = ((-1, 0), (1, 0), (0, -1), (0, 1), (-1, -1), (-1, 1), (1, -1), (1, 1))


def iota(shape, dim):
    return lax.broadcasted_iota(jnp.int32, shape, dim)


def split3(x):
    high = x.astype(BF16)
    rest = x - high.astype(F32)
    mid = rest.astype(BF16)
    low = (rest - mid.astype(F32)).astype(BF16)
    return jnp.concatenate([high, mid, low], axis=0)


def dot3(x, ones):
    rows = x.shape[0]
    y = jnp.dot(split3(x), ones, preferred_element_type=F32)
    return y[:rows] + y[rows : 2 * rows] + y[2 * rows :]


def one_zero(mask):
    return jnp.where(mask, 1.0, 0.0).astype(BF16)


class Tile:
    tiers = range(4)

    @staticmethod
    def part(ref, t, row, size):
        return ref[t, :, pl.ds(row, size), :]

    @staticmethod
    def put(ref, t, row, size, value):
        ref[t, :, pl.ds(row, size), :] = value

    @staticmethod
    def slot(ref, k, t):
        return ref[k, t]

    @staticmethod
    def put_slot(ref, k, t, value):
        ref[k, t] = value

    @staticmethod
    def left(x):
        lane = iota(x.shape, 2)
        y = pltpu.roll(x, 1, 2)
        return jnp.where(lane == 0, jnp.concatenate([y[3:], y[:3]], axis=0), y)

    @staticmethod
    def right(x):
        lane = iota(x.shape, 2)
        y = pltpu.roll(x, 127, 2)
        return jnp.where(lane == 127, jnp.concatenate([y[1:], y[:1]], axis=0), y)

    @staticmethod
    def vertical(read, v, x, t):
        if t == 0:
            return read(v, 0) * read(x, 1)
        if t == 3:
            return read(v, 2) * read(x, 2)
        return read(v, t) * read(x, t + 1) + read(v, t - 1) * read(x, t - 1)

    @staticmethod
    def via_sum(read, v, t):
        if t == 0:
            return read(v, 0)
        if t == 3:
            return read(v, 2)
        return read(v, t) + read(v, t - 1)

    @staticmethod
    def drops(read, v, x, t):
        total = None
        for low in (t - 1, t):
            if 0 <= low < 3:
                e = read(x, low) - read(x, low + 1)
                e = read(v, low) * (e * e)
                total = e if total is None else total + e
        return total


class Strip:
    tiers = (0,)

    @staticmethod
    def part(ref, t, row, size):
        return ref[pl.ds(row, size), :]

    @staticmethod
    def put(ref, t, row, size, value):
        ref[pl.ds(row, size), :] = value

    @staticmethod
    def slot(ref, k, t):
        return ref[k]

    @staticmethod
    def put_slot(ref, k, t, value):
        ref[k] = value

    @staticmethod
    def left(x):
        return pltpu.roll(x, 1, 1)

    @staticmethod
    def right(x):
        return pltpu.roll(x, 127, 1)

    @staticmethod
    def vertical(read, v, x, t):
        vm, xm = read(v, t), read(x, t)
        return vm * pltpu.roll(xm, 96, 1) + pltpu.roll(vm * xm, 32, 1)

    @staticmethod
    def via_sum(read, v, t):
        vm = read(v, t)
        return vm + pltpu.roll(vm, 32, 1)

    @staticmethod
    def drops(read, v, x, t):
        xm = read(x, t)
        e = xm - pltpu.roll(xm, 96, 1)
        e = read(v, t) * (e * e)
        return e + pltpu.roll(e, 32, 1)


class Domain:
    def __init__(self, kind, g, j, v, inv, gr, slots, x, w, power):
        self.kind, self.g, self.j, self.v, self.inv = kind, g, j, v, inv
        self.lr, self.lg, self.lw = slots
        self.gr, self.x, self.w, self.power = gr, x, w, power

    def lateral(self, p, row, size, slot):
        kind = self.kind
        for t in kind.tiers:
            if p == 3:
                x = kind.part(self.x[3], t, row, size)
                kind.put_slot(self.lw, slot, t, kind.right(x))
                continue
            w = kind.part(self.w[p], t, row, size)
            kind.put_slot(self.lw, slot, t, kind.left(w) + kind.right(w))
            if p == 0:
                g = kind.part(self.g, t, row, size)
                right = kind.right(g)
                kind.put_slot(self.lr, slot, t, right)
                kind.put_slot(self.lg, slot, t, kind.left(g) + right)

    def sweep(self, p, row, size, slot):
        kind, g, v = self.kind, self.g, self.v
        x, w = self.x[min(p, 3)], self.w
        for t in kind.tiers:
            read = lambda ref, t=t, k=0: kind.part(ref, t, row + k, size)
            put = lambda ref, value, t=t: kind.put(ref, t, row, size, value)
            gm, xm = read(g, t), read(x, t)
            if p == 3:
                right = xm - kind.slot(self.lw, slot, t)
                put(self.power[1], gm * (read(self.gr, t) * (right * right)))
                down = xm - read(x, t, 1)
                e = gm * (read(g, t, 1) * (down * down))
                put(self.power[2], e)
                node = (LEAK * xm) * xm + 0.5 * kind.drops(read, v, x, t)
                put(self.power[0], node + e)
                continue
            near = read(w[p], t, -1) + read(w[p], t, 1) + kind.slot(self.lw, slot, t)
            near = read(self.j, t) + gm * near + kind.vertical(read, v, x, t)
            if p == 0:
                near_g = read(g, t, -1) + read(g, t, 1) + kind.slot(self.lg, slot, t)
                inv = 1.0 / ((LEAK + gm * near_g) + kind.via_sum(read, v, t))
                new = inv * near
                put(self.inv, inv)
                put(self.gr, kind.slot(self.lr, slot, t))
            else:
                a, b = STEP_1 if p == 1 else STEP_2
                new = (1.0 + a - b) * xm - a * read(self.x[p - 1], t)
                new = new + b * (read(self.inv, t) * near)
            put(self.x[p + 1], new)
            if p < 2:
                put(w[p + 1], gm * new)


def solve(passes, steps, unroll, *parts):
    for p in passes:
        for domain, row, size in parts:
            domain.lateral(p, row, size, 0)

        def one(n, carry):
            for k in range(unroll):
                for domain, row, size in parts:
                    now = row + k * size
                    if steps > unroll:
                        now = now + pl.multiple_of(n * (unroll * size), unroll * size)
                    domain.sweep(p, now, size, k)
                    if steps > unroll or k + 1 < unroll:
                        domain.lateral(p, now + size, size, (k + 1) % unroll)
            return carry

        if steps > unroll:
            lax.fori_loop(0, steps // unroll, one, 0)
        else:
            one(0, 0)


def lane32(shape):
    return (iota(shape, 1) + 20) % 32


def pack_edges(tiers):
    shape = tiers[0][0].shape
    group = ((iota(shape, 1) + 12) // 32) % 4
    out = jnp.zeros(shape, F32)
    for t, (first, last) in enumerate(tiers):
        ends = first if first is last else jnp.where(iota(shape, 1) < 64, first, last)
        if t:
            ends = pltpu.roll(ends, 32 * t, 1)
        out = jnp.where(group == t, ends, out)
    return jnp.where(lane32(shape) >= 16, out, pltpu.roll(out, 120, 1))


def unpack_edges(packed, tiers):
    ends = jnp.where(lane32(packed.shape) >= 20, packed, pltpu.roll(packed, 8, 1))
    return [pltpu.roll(ends, (-32 * t) % 128, 1) if t else ends for t in range(tiers)]


def with_sides(mid, from_left, from_right):
    l32 = lane32(mid.shape)
    mid = jnp.where((l32 >= 16) & (l32 < 20), pltpu.roll(from_left, 8, 1), mid)
    return jnp.where((l32 >= 12) & (l32 < 16), pltpu.roll(from_right, 120, 1), mid)


def kernel(
    n_row, n_col,
    v_h, a_h, t_h, vi_h, fe_h, in_h,
    x3, tt, ht, tl, hl,
    x, x1, x2, g, j, v, inv, gr, lr, lg, lw, wa, wb, wc, p0, p1, p2,
    expand, x_raw, a_raw, vi_raw, fe_raw, in_raw, t_raw,
    qx, qx1, qx2, qx3, qg, qj, qv, qi, qgr, qlr, qlg, qlw, qa, qb, qc, q0, q1, q2,
    ra_s, ra_r, rb_s, rb_r, cm_s, cm_r, cr_r,
    load, r2_s, r2_r, c2_s, c2_r, k2_r, ts, tu, hs, hu, pick, pick_ends,
    in_sem, send_sem, recv_sem, send2_sem, recv2_sem,
):
    row = lax.axis_index("row")
    col = lax.axis_index("col")

    def there(dr, dc):
        ok = None
        for cond in (
            (row > 0) if dr < 0 else (row < n_row - 1) if dr > 0 else None,
            (col > 0) if dc < 0 else (col < n_col - 1) if dc > 0 else None,
        ):
            if cond is not None:
                ok = cond if ok is None else jnp.logical_and(ok, cond)
        return ok

    def device(dr, dc):
        return {"row": row + dr, "col": col + dc}

    barrier = pltpu.get_barrier_semaphore()
    for dr, dc in DIRS:

        @pl.when(there(dr, dc))
        def _(dr=dr, dc=dc):
            pl.semaphore_signal(
                barrier, inc=1, device_id=device(dr, dc), device_id_type=MESH
            )

    copies = {}
    slot = 0

    def fetch(name, src, dst):
        nonlocal slot
        copy = pltpu.make_async_copy(src, dst, in_sem.at[slot])
        slot += 1
        copy.start()
        copies.setdefault(name, []).append(copy)

    fetch("t", t_h, t_raw)
    inputs = ((a_h, a_raw), (v_h, x_raw), (fe_h, fe_raw), (in_h, in_raw), (vi_h, vi_raw))
    for name, first, size in (
        ("outer", 0, 8),
        ("outer", ROWS - 8, 8),
        ("inner", 8, ROWS - 16),
    ):
        for src, dst in inputs:
            rows = pl.ds(first, size)
            fetch(name, src.at[:, rows, :], dst.at[:, rows, :])

    def arrived(*names):
        for name in names:
            for copy in copies[name]:
                copy.wait()

    for ref in (x3, g, wa, wb, wc):
        for start in (0, M0 + ROWS, S0 + 24):
            ref[:, :, pl.ds(start, 8), :] = jnp.zeros((4, 4, 8, 128), F32)
    for ref in (qx, qx3, qg, qj, qv, qa, qb, qc):
        for start in (0, Q0 + ROWS):
            ref[pl.ds(start, 16), :] = jnp.zeros((16, 128), F32)
    for ref in (ts, tu):
        for start in (0, 48):
            ref[:, pl.ds(start, 8), :] = jnp.zeros((4, 8, 128), F32)
    for ref in (hs, hu):
        for start in (0, 48):
            ref[pl.ds(start, 8), :] = jnp.zeros((8, 128), F32)
    for s in range(2):
        rb_s[s, pl.ds(16, 8), :] = jnp.zeros((8, 128), F32)
        r2_s[s, pl.ds(0, 8), :] = jnp.zeros((8, 128), F32)

        @pl.when(jnp.logical_not(there(*DIRS[s])))
        def _(s=s):
            ra_r[s] = jnp.zeros((15, 2, 8, 128), F32)
            rb_r[s] = jnp.zeros((40, 128), F32)
            r2_r[s] = jnp.zeros((24, 128), F32)

        @pl.when(jnp.logical_not(there(*DIRS[2 + s])))
        def _(s=s):
            cm_r[s] = jnp.zeros((96, 128), F32)
            c2_r[s] = jnp.zeros((32, 128), F32)

    for s in range(4):

        @pl.when(jnp.logical_not(there(*DIRS[4 + s])))
        def _(s=s):
            cr_r[s] = jnp.zeros((24, 128), F32)
            k2_r[s] = jnp.zeros((8, 128), F32)

    node, cell = iota((256, 128), 0), iota((256, 128), 1)
    inner = (cell > 0) & (cell < 127)
    for h in range(2):
        own = inner & (node // 4 + 64 * h == cell)
        after = inner & (node // 4 + 64 * h + 1 == cell)
        last = node % 4 == 3
        pick[h, 0] = one_zero(own)
        pick[h, 1] = jnp.where(
            (own | after) & last, 0.5, jnp.where(own, 1.0, 0.0)
        ).astype(BF16)
    start_lane = jnp.where(cell % 32 == 0, cell, cell - 11)
    place = (node - start_lane + 1) % 128 - 1
    edge = (cell % 32 == 0) | (cell % 32 == 31)
    whole = edge & (place >= 0) & (place < 4)
    halved = edge & (node >= 128) & ((place == -1) | (place == 3))
    pick_ends[...] = jnp.where(halved, 0.5, jnp.where(whole, 1.0, 0.0)).astype(BF16)

    arrived("t")
    cells = jnp.exp(-0.25 * t_raw[...]).reshape(128, 128)
    wide = iota((128, 512), 1) // 4 == iota((128, 512), 0)
    fine = dot3(cells, one_zero(wide))
    for b in range(4):
        part = fine[:, 128 * b : 128 * (b + 1)].reshape(4, 32, 128)
        for k in range(4):
            expand[:, b, pl.ds(k, 32, 4), :] = part

    arrived("outer")

    def prepare(off):
        raw, rows = pl.ds(off, 8), pl.ds(M0 + off, 8)
        for t in range(4):
            for b in range(4):
                lanes = slice(128 * b, 128 * (b + 1))
                adm, old = a_raw[t, raw, lanes], x_raw[t, raw, lanes]
                gm = adm * lax.rsqrt(adm) * expand[t, b, raw, :]
                g[t, b, rows, :] = gm
                x[t, b, rows, :] = old
                wa[t, b, rows, :] = gm * old
                j[t, b, rows, :] = fe_raw[t, raw, lanes].astype(F32) * in_raw[t, raw, lanes]
                if t < 3:
                    v[t, b, rows, :] = vi_raw[t, raw, lanes].astype(F32)

    def remote(src, dst, send, recv, dr, dc):
        return pltpu.make_async_remote_copy(
            src_ref=src,
            dst_ref=dst,
            send_sem=send,
            recv_sem=recv,
            device_id=device(dr, dc),
            device_id_type=MESH,
        )

    nodes = ((x, 4), (g, 4), (j, 4), (v, 3))
    strips = (qx, qg, qj, qv)

    prepare(0)
    prepare(ROWS - 8)
    for s, first in ((0, 0), (1, ROWS - 4)):
        for k, (ref, tiers) in enumerate(nodes):
            for h in range(2):
                ra_s[s, pl.ds(4 * k, tiers), :, pl.ds(4 * h, 4), :] = ref[
                    :, pl.ds(2 * h, 2), pl.ds(M0 + first, 4), :
                ]

    neighbours = 0
    for dr, dc in DIRS:
        neighbours = neighbours + there(dr, dc).astype(jnp.int32)
    pl.semaphore_wait(barrier, neighbours)

    row_exchange, first_exchange = [], []
    for s in range(2):
        row_exchange.append((DIRS[s], ra_s.at[s], ra_r.at[1 - s], s, 1 - s))
        first_exchange.append((DIRS[s], rb_s.at[s], rb_r.at[1 - s], 2 + s, 3 - s))
    for s in range(4):
        first_exchange.append(
            (DIRS[4 + s], rb_s.at[s // 2, pl.ds(0, 24)], cr_r.at[3 - s], 6 + s, 9 - s)
        )
    for s in range(2):
        first_exchange.append((DIRS[2 + s], cm_s.at[s], cm_r.at[1 - s], 4 + s, 5 - s))
    second_exchange = []
    for s in range(2):
        second_exchange.append((DIRS[s], r2_s.at[s], r2_r.at[1 - s], s, 1 - s))
        second_exchange.append((DIRS[2 + s], c2_s, c2_r.at[1 - s], 2 + s, 3 - s))
    for s in range(4):
        second_exchange.append(
            (DIRS[4 + s], r2_s.at[s // 2, pl.ds(0, 8)], k2_r.at[3 - s], 4 + s, 7 - s)
        )

    def start(exchange, sends, recvs):
        for (dr, dc), src, dst, a, b in exchange:

            @pl.when(there(dr, dc))
            def _(dr=dr, dc=dc, src=src, dst=dst, a=a, b=b):
                remote(src, dst, sends.at[a], recvs.at[b], dr, dc).start()

    def wait_recv(exchange, sends, recvs):
        for (dr, dc), src, dst, a, b in exchange:

            @pl.when(there(-dr, -dc))
            def _(dr=dr, dc=dc, src=src, dst=dst, a=a, b=b):
                remote(src, dst, sends.at[a], recvs.at[b], -dr, -dc).wait_recv()

    def wait_send(exchange, sends, recvs):
        for (dr, dc), src, dst, a, b in exchange:

            @pl.when(there(dr, dc))
            def _(dr=dr, dc=dc, src=src, dst=dst, a=a, b=b):
                remote(src, dst, sends.at[a], recvs.at[b], dr, dc).wait_send()

    start(row_exchange, send_sem, recv_sem)
    arrived("inner")

    def prepare_more(n, carry):
        prepare(pl.multiple_of(n * 8, 8))
        return carry

    lax.fori_loop(1, ROWS // 8 - 1, prepare_more, 0, unroll=2)

    tile = pl.ds(M0, ROWS)
    for (ref, tiers), packed in zip(nodes, strips):
        packed[pl.ds(Q0, ROWS), :] = pack_edges(
            [(ref[t, 0, tile, :], ref[t, 3, tile, :]) for t in range(tiers)]
        )
    t_edges = pack_edges([(t_raw[t], t_raw[t]) for t in range(4)])
    for s, first in ((0, 0), (1, ROWS - 4)):
        for k, packed in enumerate(strips):
            rb_s[s, pl.ds(4 * k, 4), :] = packed[pl.ds(Q0 + first, 4), :]
        cell = 0 if s == 0 else 28
        rb_s[s, pl.ds(16, 4), :] = t_edges[cell : cell + 4]
        for t in range(4):
            rb_s[s, pl.ds(24 + 4 * t, 4), :] = t_raw[t, pl.ds(cell, 4), :]
    group = lane32((64, 128)) // 4
    for s, lane0 in ((0, 20), (1, 8)):
        mixed = jnp.zeros((64, 128), F32)
        for k, packed in enumerate(strips):
            for h in range(2):
                slot32 = h * 16 + k * 4
                part = packed[pl.ds(Q0 + 64 * h, 64), :]
                if slot32 != lane0:
                    part = pltpu.roll(part, (slot32 - lane0) % 128, 1)
                mixed = jnp.where(group == slot32 // 4, part, mixed)
        cm_s[s, pl.ds(0, 64), :] = mixed
        cm_s[s, pl.ds(64, 32), :] = t_edges
    start(first_exchange, send_sem, recv_sem)

    for ref, _ in nodes:
        ref[:, :, pl.ds(S0 + 4, 8), :] = ref[:, :, pl.ds(M0, 8), :]
        ref[:, :, pl.ds(S0 + 12, 8), :] = ref[:, :, pl.ds(M0 + ROWS - 8, 8), :]

    big = Domain(
        Tile, g, j, v, inv, gr, (lr, lg, lw), (x, x1, x2, x3), (wa, wb, wc), (p0, p1, p2)
    )
    side = Domain(
        Strip, qg, qj, qv, qi, qgr, (qlr, qlg, qlw),
        (qx, qx1, qx2, qx3), (qa, qb, qc), (q0, q1, q2),
    )
    solve(range(4), ROWS // 8, MAIN_UNROLL, (big, M0, 8))

    wait_recv(row_exchange, send_sem, recv_sem)
    wait_recv(first_exchange, send_sem, recv_sem)

    for s, first in ((0, 0), (1, 20)):
        for k, (ref, tiers) in enumerate(nodes):
            for h in range(2):
                ref[:, pl.ds(2 * h, 2), pl.ds(S0 + first, 4), :] = ra_r[
                    s, pl.ds(4 * k, tiers), :, pl.ds(4 * h, 4), :
                ]
    strip = pl.ds(S0, 24)
    wa[:, :, strip, :] = g[:, :, strip, :] * x[:, :, strip, :]

    l32 = lane32((64, 128))
    for k, packed in enumerate(strips):
        for s, first in ((0, Q0 - 4), (1, Q0 + ROWS)):
            part = pl.ds(4 * k, 4)
            packed[pl.ds(first, 4), :] = with_sides(
                rb_r[s, part, :], cr_r[2 * s, part, :], cr_r[2 * s + 1, part, :]
            )
        for h in range(2):
            rows = pl.ds(Q0 + 64 * h, 64)
            slot32 = h * 16 + k * 4
            mid = packed[rows, :]
            for s, lane0 in ((0, 16), (1, 12)):
                part = cm_r[s, pl.ds(0, 64), :]
                if slot32 != lane0:
                    part = pltpu.roll(part, (lane0 - slot32) % 128, 1)
                mid = jnp.where((l32 >= lane0) & (l32 < lane0 + 4), part, mid)
            packed[rows, :] = mid
    strip = pl.ds(8, 144)
    qa[strip, :] = qg[strip, :] * qx[strip, :]
    solve(range(4), 3, STRIP_UNROLL, (big, S0, 8), (side, 8, 48))

    for ref, before in ((p0, 0), (p1, 0), (p2, 1)):
        ref[:, :, pl.ds(M0 - before, 4 + before), :] = ref[
            :, :, pl.ds(S0 + 4 - before, 4 + before), :
        ]
        ref[:, :, pl.ds(M0 + ROWS - 4, 4), :] = ref[:, :, pl.ds(S0 + 16, 4), :]

    def cell_rows(parts, first):
        take = lambda ref, k: ref[
            (slice(None),) * (len(ref.shape) - 2) + (pl.ds(first + k, 32, 4), slice(None))
        ]
        total = 0.5 * (take(parts[2], -1) - take(parts[2], 3))
        right = take(parts[1], 0)
        for k in range(4):
            total = total + take(parts[0], k)
            if k:
                right = right + take(parts[1], k)
        return total, right

    sums, rights = cell_rows(big.power, M0)
    edge_sums, edge_rights = cell_rows(side.power, Q0)
    total = jnp.zeros((128, 128), F32)
    for h in range(2):
        for k, values in enumerate((sums, rights)):
            both = jnp.concatenate(
                [values[:, 2 * h].reshape(128, 128), values[:, 2 * h + 1].reshape(128, 128)],
                axis=1,
            )
            total = total + dot3(both, pick[h, k])
    ends = dot3(jnp.concatenate([edge_sums, edge_rights], axis=1), pick_ends[...])
    lane = iota((32, 128), 1)
    for t in range(4):
        mine = pltpu.roll(ends, (-32 * t) % 128, 1) if t else ends
        mine = jnp.where((lane == 0) | (lane == 127), mine, total[32 * t : 32 * (t + 1)])
        load[t] = GAIN * mine

    l_edges = pack_edges([(load[t], load[t]) for t in range(4)])
    c2_s[...] = l_edges
    for s, cell in ((0, 0), (1, 28)):
        r2_s[s, pl.ds(0, 4), :] = l_edges[cell : cell + 4]
        for t in range(4):
            r2_s[s, pl.ds(8 + 4 * t, 4), :] = load[t, pl.ds(cell, 4), :]
    start(second_exchange, send2_sem, recv2_sem)

    x3[:, :, pl.ds(M0, 4), :] = x3[:, :, pl.ds(S0 + 4, 4), :]
    x3[:, :, pl.ds(M0 + ROWS - 4, 4), :] = x3[:, :, pl.ds(S0 + 16, 4), :]
    lane = iota((ROWS, 128), 1)
    for t, ends in enumerate(unpack_edges(qx3[pl.ds(Q0, ROWS), :], 4)):
        x3[t, 0, tile, :] = jnp.where(lane < 4, ends, x3[t, 0, tile, :])
        x3[t, 3, tile, :] = jnp.where(lane >= 124, ends, x3[t, 3, tile, :])

    for t in range(4):
        tt[t, pl.ds(0, 4), :] = rb_r[0, pl.ds(24 + 4 * t, 4), :]
        tt[t, pl.ds(4, 32), :] = t_raw[t]
        tt[t, pl.ds(36, 4), :] = rb_r[1, pl.ds(24 + 4 * t, 4), :]
    cells = pl.ds(64, 32)
    edge = pl.ds(16, 4)
    ht[pl.ds(0, 4), :] = with_sides(rb_r[0, edge, :], cr_r[0, edge, :], cr_r[1, edge, :])
    ht[pl.ds(4, 32), :] = with_sides(t_edges, cm_r[0, cells, :], cm_r[1, cells, :])
    ht[pl.ds(36, 4), :] = with_sides(rb_r[1, edge, :], cr_r[2, edge, :], cr_r[3, edge, :])
    heat_of = Heat(n_row, n_col, ts, tu, hs, hu)
    theta, side = tt[...], ht[...]
    tt[...] = theta + DT * heat_of.tile(theta)
    ht[...] = side + DT * heat_of.strip(side)

    wait_recv(second_exchange, send2_sem, recv2_sem)
    for t in range(4):
        tl[t, pl.ds(0, 4), :] = r2_r[0, pl.ds(8 + 4 * t, 4), :]
        tl[t, pl.ds(4, 32), :] = load[t]
        tl[t, pl.ds(36, 4), :] = r2_r[1, pl.ds(8 + 4 * t, 4), :]
    edge = pl.ds(0, 4)
    hl[pl.ds(0, 4), :] = with_sides(r2_r[0, edge, :], k2_r[0, edge, :], k2_r[1, edge, :])
    hl[pl.ds(4, 32), :] = with_sides(l_edges, c2_r[0], c2_r[1])
    hl[pl.ds(36, 4), :] = with_sides(r2_r[1, edge, :], k2_r[2, edge, :], k2_r[3, edge, :])

    wait_send(row_exchange, send_sem, recv_sem)
    wait_send(first_exchange, send_sem, recv_sem)
    wait_send(second_exchange, send2_sem, recv2_sem)


class Heat:
    def __init__(self, n_row, n_col, ts, tu, hs, hu):
        row, col = lax.axis_index("row"), lax.axis_index("col")
        self.refs = (ts, tu, hs, hu)
        r, l32 = iota((40, 128), 0), lane32((40, 128))
        rows_in = ((r >= 4) | (row > 0)) & ((r < 36) | (row < n_row - 1))
        cols_in = ((l32 < 16) | (l32 >= 20) | (col > 0)) & (
            (l32 < 12) | (l32 >= 16) | (col < n_col - 1)
        )
        tier = ((iota((40, 128), 1) + 20) // 32) % 4
        real = lambda mask: jnp.where(mask, 1.0, 0.0).astype(F32)
        self.row_mask, self.all_mask = real(rows_in), real(rows_in & cols_in)
        self.not_first, self.not_last = real(tier > 0), real(tier < 3)

    @staticmethod
    def flux(theta, s, u, s_ref, u_ref, rows, axis):
        def near(ref, mid):
            around = ref[rows(7)] + ref[rows(9)]
            return around + pltpu.roll(mid, 1, axis) + pltpu.roll(mid, 127, axis)

        s_ref[rows(8)] = s
        u_ref[rows(8)] = u
        return s * (near(u_ref, u) - theta * near(s_ref, s))

    def tile(self, theta):
        s = jnp.exp(-0.15 * theta) * self.row_mask
        rows = lambda k: (slice(None), pl.ds(k, 40), slice(None))
        flux = self.flux(theta, s, s * theta, *self.refs[:2], rows, 2)
        vert = jnp.concatenate(
            [
                theta[1:2] - theta[0:1],
                theta[0:2] + theta[2:4] - 2.0 * theta[1:3],
                theta[2:3] - 2.0 * theta[3:4],
            ],
            axis=0,
        )
        return flux + vert

    def strip(self, theta):
        s = jnp.exp(-0.15 * theta) * self.all_mask
        rows = lambda k: (pl.ds(k, 40), slice(None))
        flux = self.flux(theta, s, s * theta, *self.refs[2:], rows, 1)
        vert = (
            self.not_last * pltpu.roll(theta, 96, 1)
            + self.not_first * pltpu.roll(theta, 32, 1)
            - (1.0 + self.not_first) * theta
        )
        return flux + vert


def finish(
    n_row, n_col, x3, tt, ht, tl, hl, xo_h, to_h, ts, tu, hs, hu, t_out, out_sem
):
    copies = []
    for b in range(4):
        copy = pltpu.make_async_copy(
            x3.at[:, b, pl.ds(M0, ROWS), :], xo_h.at[:, :, pl.ds(128 * b, 128)], out_sem.at[b]
        )
        copy.start()
        copies.append(copy)
    for ref in (ts, tu):
        for start in (0, 48):
            ref[:, pl.ds(start, 8), :] = jnp.zeros((4, 8, 128), F32)
    for ref in (hs, hu):
        for start in (0, 48):
            ref[pl.ds(start, 8), :] = jnp.zeros((8, 128), F32)
    heat_of = Heat(n_row, n_col, ts, tu, hs, hu)
    heat, side_heat = tl[...], hl[...]
    theta, side = tt[...] + DT * heat, ht[...] + DT * side_heat
    for _ in range(HEAT_SWEEPS - 1):
        gain, side_gain = heat_of.tile(theta), heat_of.strip(side)
        theta = theta + DT * (gain + heat)
        side = side + DT * (side_gain + side_heat)
    lane = iota((32, 128), 1)
    for t, ends in enumerate(unpack_edges(side[4:36], 4)):
        t_out[t] = jnp.where((lane < 4) | (lane >= 124), ends, theta[t, 4:36])
    copy = pltpu.make_async_copy(t_out, to_h, out_sem.at[4])
    copy.start()
    copies.append(copy)
    for copy in copies:
        copy.wait()


def vmem(*shape, dtype=F32):
    return pltpu.VMEM(shape, dtype)


def on_device(n_row, n_col, *args):
    node = (4, 4, R_ALL, 128)
    raw = (4, ROWS, 512)
    strip = (Q_ALL, 128)
    heat = [vmem(4, 56, 128), vmem(4, 56, 128), vmem(56, 128), vmem(56, 128)]
    scratch = [
        *[vmem(*node) for _ in range(5)], vmem(3, *node[1:]),
        *[vmem(*node) for _ in range(2)],
        *[vmem(MAIN_UNROLL, 4, 4, 8, 128) for _ in range(3)],
        *[vmem(*node) for _ in range(6)],
        vmem(4, 4, ROWS, 128), vmem(*raw), vmem(*raw), vmem(3, *raw[1:], dtype=jnp.int32),
        vmem(*raw, dtype=jnp.int32), vmem(*raw), vmem(4, 32, 128),
        *[vmem(*strip) for _ in range(9)],
        *[vmem(STRIP_UNROLL, 48, 128) for _ in range(3)],
        *[vmem(*strip) for _ in range(6)],
        vmem(2, 15, 2, 8, 128), vmem(2, 15, 2, 8, 128),
        vmem(2, 40, 128), vmem(2, 40, 128),
        vmem(2, 96, 128), vmem(2, 96, 128),
        vmem(4, 24, 128),
        vmem(4, 32, 128),
        vmem(2, 24, 128), vmem(2, 24, 128),
        vmem(32, 128), vmem(2, 32, 128),
        vmem(4, 8, 128),
        *heat,
        vmem(2, 2, 256, 128, dtype=BF16), vmem(256, 128, dtype=BF16),
        pltpu.SemaphoreType.DMA((16,)),
        pltpu.SemaphoreType.DMA((10,)),
        pltpu.SemaphoreType.DMA((10,)),
        pltpu.SemaphoreType.DMA((8,)),
        pltpu.SemaphoreType.DMA((8,)),
    ]
    hbm = pl.BlockSpec(memory_space=pltpu.HBM)
    local = pl.BlockSpec(memory_space=pltpu.VMEM)
    mids = pl.pallas_call(
        functools.partial(kernel, n_row, n_col),
        out_shape=tuple(
            pltpu.VMEM(shape, F32)
            for shape in (node, (4, 40, 128), (40, 128), (4, 40, 128), (40, 128))
        ),
        in_specs=[hbm] * 6,
        out_specs=(local,) * 5,
        scratch_shapes=scratch,
        compiler_params=pltpu.CompilerParams(
            collective_id=0,
            has_side_effects=True,
            vmem_limit_bytes=56 * 1024 * 1024,
        ),
    )(*[pltpu.with_memory_space_constraint(arg, pltpu.HBM) for arg in args])
    return pl.pallas_call(
        functools.partial(finish, n_row, n_col),
        out_shape=(
            jax.ShapeDtypeStruct((4, ROWS, 512), F32),
            jax.ShapeDtypeStruct((4, 32, 128), F32),
        ),
        in_specs=[local] * 5,
        out_specs=(hbm, hbm),
        scratch_shapes=[*heat, vmem(4, 32, 128), pltpu.SemaphoreType.DMA((5,))],
        compiler_params=pltpu.CompilerParams(vmem_limit_bytes=4 * 1024 * 1024),
    )(*mids)


def solution(mesh):
    spec = P(None, "row", "col")
    return jax.shard_map(
        functools.partial(on_device, mesh.shape["row"], mesh.shape["col"]),
        mesh=mesh,
        in_specs=(spec,) * 6,
        out_specs=(spec, spec),
        check_vma=False,
    )
```

profile of v0, /device:TPU:1, one launch (start us, length us, event | category | flops | bytes accessed | tf_op | source)
XLA Modules:
  0.0 20.6 jit_solution(5198847016591923855)
XLA Ops:
  0.6 18.6 %shard_map.77 = (f32[4,4,176,128]{3,2,1,0:T(8,128)S(1)}, f32[4,40,128]{2,1,0:T(8,128)S(1)}, f32[40,128]{1,0:T(8,128)S(1)}, f32[4,40,128]{2,1,0:T(8,128)S(1)}, f32[40,128]{1,0:T(8,128)S(1)}) custom-call(f32[4,128,512]{2,1,0:T(8,128)} %v_h.1, f32[4,128,512]{2,1,0:T(8,128)} %a_h.1, f32[4,32,128]{2,1,0:T(8,128)} %t_h.1, s32[3,128,512]{2,1,0:T(8,128)} %vi_h.1, ...), custom_call_target="tpu_custom_call" | custom-call | tf_op jit(solution)/shard_map/pallas_call | solution.py:752
  19.2 1.3 %shard_map.78 = (f32[4,128,512]{2,1,0:T(8,128)}, f32[4,32,128]{2,1,0:T(8,128)}) custom-call(f32[4,4,176,128]{3,2,1,0:T(8,128)S(1)} %get-tuple-element.7.x3, f32[4,40,128]{2,1,0:T(8,128)S(1)} %get-tuple-element.8.tt, f32[40,128]{1,0:T(8,128)S(1)} %get-tuple-element.9.ht, f32[4,40,128]{2,1,0:T(8,128)S(1)} %get-tuple-element.10.tl, ...), custom_call_target="tpu_custom_call" | custom-call | tf_op jit(solution)/shard_map/pallas_call | solution.py:767
where the time goes:
time: 20.7 us; the launch traced here: 20.6 us
  Pallas kernels  19.9 us (96%)
  between operations  0.64 us (3%)
    pallas_call x1, Pallas kernels, on_device(): pl.pallas_call(functools.partial(kernel, n_row, n_col), out_shape=tuple((...  18.6 us
    pallas_call x1, Pallas kernels, on_device(): pl.pallas_call(functools.partial(finish, n_row, n_col), out_shape=(jax.Sh...  1.33 us

commit v1 on v0

--- a/solution.py
+++ b/solution.py
@@ -24,6 +24,8 @@
 GAIN = 0.0625
 MAIN_UNROLL = 4
 STRIP_UNROLL = 3
+GROUPS = 4
+GROUP = 32
 
 ROWS = 128
 M0 = 8
@@ -257,6 +259,30 @@
     return [pltpu.roll(ends, (-32 * t) % 128, 1) if t else ends for t in range(tiers)]
 
 
+def squeeze(edges, lane0):
+    slot = lane32((8, 128)) // 4
+    out = jnp.zeros((8, 128), F32)
+    for q in range(4):
+        part = edges[8 * q : 8 * q + 8]
+        if 4 * q != lane0:
+            part = pltpu.roll(part, (4 * q - lane0) % 128, 1)
+        out = jnp.where(slot == q, part, out)
+    return out
+
+
+def with_squeezed_sides(mid, from_left, from_right):
+    l32 = lane32((8, 128))
+    rows = []
+    for q in range(4):
+        part = mid[8 * q : 8 * q + 8]
+        for lane0, side in ((16, from_left), (12, from_right)):
+            if 4 * q != lane0:
+                side = pltpu.roll(side, (lane0 - 4 * q) % 128, 1)
+            part = jnp.where((l32 >= lane0) & (l32 < lane0 + 4), side, part)
+        rows.append(part)
+    return jnp.concatenate(rows, axis=0)
+
+
 def with_sides(mid, from_left, from_right):
     l32 = lane32(mid.shape)
     mid = jnp.where((l32 >= 16) & (l32 < 20), pltpu.roll(from_left, 8, 1), mid)
@@ -271,7 +297,7 @@
     expand, x_raw, a_raw, vi_raw, fe_raw, in_raw, t_raw,
     qx, qx1, qx2, qx3, qg, qj, qv, qi, qgr, qlr, qlg, qlw, qa, qb, qc, q0, q1, q2,
     ra_s, ra_r, rb_s, rb_r, cm_s, cm_r, cr_r,
-    load, r2_s, r2_r, c2_s, c2_r, k2_r, ts, tu, hs, hu, pick, pick_ends,
+    load, r2_s, r2_r, c2_s, c2_r, k2_s, k2_r, ts, tu, hs, hu, pick, pick_ends,
     in_sem, send_sem, recv_sem, send2_sem, recv2_sem,
 ):
     row = lax.axis_index("row")
@@ -311,14 +337,10 @@
 
     fetch("t", t_h, t_raw)
     inputs = ((a_h, a_raw), (v_h, x_raw), (fe_h, fe_raw), (in_h, in_raw), (vi_h, vi_raw))
-    for name, first, size in (
-        ("outer", 0, 8),
-        ("outer", ROWS - 8, 8),
-        ("inner", 8, ROWS - 16),
-    ):
+    for n in range(GROUPS):
         for src, dst in inputs:
-            rows = pl.ds(first, size)
-            fetch(name, src.at[:, rows, :], dst.at[:, rows, :])
+            rows = pl.ds(n * GROUP, GROUP)
+            fetch(n, src.at[:, rows, :], dst.at[:, rows, :])
 
     def arrived(*names):
         for name in names:
@@ -339,18 +361,18 @@
             ref[pl.ds(start, 8), :] = jnp.zeros((8, 128), F32)
     for s in range(2):
         rb_s[s, pl.ds(16, 8), :] = jnp.zeros((8, 128), F32)
-        r2_s[s, pl.ds(0, 8), :] = jnp.zeros((8, 128), F32)
+        k2_s[s] = jnp.zeros((8, 128), F32)
 
         @pl.when(jnp.logical_not(there(*DIRS[s])))
         def _(s=s):
             ra_r[s] = jnp.zeros((15, 2, 8, 128), F32)
             rb_r[s] = jnp.zeros((40, 128), F32)
-            r2_r[s] = jnp.zeros((24, 128), F32)
+            r2_r[s] = jnp.zeros((16, 128), F32)
 
         @pl.when(jnp.logical_not(there(*DIRS[2 + s])))
         def _(s=s):
-            cm_r[s] = jnp.zeros((96, 128), F32)
-            c2_r[s] = jnp.zeros((32, 128), F32)
+            cm_r[s] = jnp.zeros((72, 128), F32)
+            c2_r[s] = jnp.zeros((8, 128), F32)
 
     for s in range(4):
 
@@ -385,8 +407,6 @@
         for k in range(4):
             expand[:, b, pl.ds(k, 32, 4), :] = part
 
-    arrived("outer")
-
     def prepare(off):
         raw, rows = pl.ds(off, 8), pl.ds(M0 + off, 8)
         for t in range(4):
@@ -414,74 +434,23 @@
     nodes = ((x, 4), (g, 4), (j, 4), (v, 3))
     strips = (qx, qg, qj, qv)
 
-    prepare(0)
-    prepare(ROWS - 8)
+    for n in range(GROUPS):
+        arrived(n)
+        for off in range(n * GROUP, (n + 1) * GROUP, 8):
+            prepare(off)
+        tile = pl.ds(M0 + n * GROUP, GROUP)
+        for (ref, tiers), packed in zip(nodes, strips):
+            packed[pl.ds(Q0 + n * GROUP, GROUP), :] = pack_edges(
+                [(ref[t, 0, tile, :], ref[t, 3, tile, :]) for t in range(tiers)]
+            )
+    tile = pl.ds(M0, ROWS)
+
     for s, first in ((0, 0), (1, ROWS - 4)):
         for k, (ref, tiers) in enumerate(nodes):
             for h in range(2):
                 ra_s[s, pl.ds(4 * k, tiers), :, pl.ds(4 * h, 4), :] = ref[
                     :, pl.ds(2 * h, 2), pl.ds(M0 + first, 4), :
                 ]
-
-    neighbours = 0
-    for dr, dc in DIRS:
-        neighbours = neighbours + there(dr, dc).astype(jnp.int32)
-    pl.semaphore_wait(barrier, neighbours)
-
-    row_exchange, first_exchange = [], []
-    for s in range(2):
-        row_exchange.append((DIRS[s], ra_s.at[s], ra_r.at[1 - s], s, 1 - s))
-        first_exchange.append((DIRS[s], rb_s.at[s], rb_r.at[1 - s], 2 + s, 3 - s))
-    for s in range(4):
-        first_exchange.append(
-            (DIRS[4 + s], rb_s.at[s // 2, pl.ds(0, 24)], cr_r.at[3 - s], 6 + s, 9 - s)
-        )
-    for s in range(2):
-        first_exchange.append((DIRS[2 + s], cm_s.at[s], cm_r.at[1 - s], 4 + s, 5 - s))
-    second_exchange = []
-    for s in range(2):
-        second_exchange.append((DIRS[s], r2_s.at[s], r2_r.at[1 - s], s, 1 - s))
-        second_exchange.append((DIRS[2 + s], c2_s, c2_r.at[1 - s], 2 + s, 3 - s))
-    for s in range(4):
-        second_exchange.append(
-            (DIRS[4 + s], r2_s.at[s // 2, pl.ds(0, 8)], k2_r.at[3 - s], 4 + s, 7 - s)
-        )
-
-    def start(exchange, sends, recvs):
-        for (dr, dc), src, dst, a, b in exchange:
-
-            @pl.when(there(dr, dc))
-            def _(dr=dr, dc=dc, src=src, dst=dst, a=a, b=b):
-                remote(src, dst, sends.at[a], recvs.at[b], dr, dc).start()
-
-    def wait_recv(exchange, sends, recvs):
-        for (dr, dc), src, dst, a, b in exchange:
-
-            @pl.when(there(-dr, -dc))
-            def _(dr=dr, dc=dc, src=src, dst=dst, a=a, b=b):
-                remote(src, dst, sends.at[a], recvs.at[b], -dr, -dc).wait_recv()
-
-    def wait_send(exchange, sends, recvs):
-        for (dr, dc), src, dst, a, b in exchange:
-
-            @pl.when(there(dr, dc))
-            def _(dr=dr, dc=dc, src=src, dst=dst, a=a, b=b):
-                remote(src, dst, sends.at[a], recvs.at[b], dr, dc).wait_send()
-
-    start(row_exchange, send_sem, recv_sem)
-    arrived("inner")
-
-    def prepare_more(n, carry):
-        prepare(pl.multiple_of(n * 8, 8))
-        return carry
-
-    lax.fori_loop(1, ROWS // 8 - 1, prepare_more, 0, unroll=2)
-
-    tile = pl.ds(M0, ROWS)
-    for (ref, tiers), packed in zip(nodes, strips):
-        packed[pl.ds(Q0, ROWS), :] = pack_edges(
-            [(ref[t, 0, tile, :], ref[t, 3, tile, :]) for t in range(tiers)]
-        )
     t_edges = pack_edges([(t_raw[t], t_raw[t]) for t in range(4)])
     for s, first in ((0, 0), (1, ROWS - 4)):
         for k, packed in enumerate(strips):
@@ -501,8 +470,55 @@
                     part = pltpu.roll(part, (slot32 - lane0) % 128, 1)
                 mixed = jnp.where(group == slot32 // 4, part, mixed)
         cm_s[s, pl.ds(0, 64), :] = mixed
-        cm_s[s, pl.ds(64, 32), :] = t_edges
+        cm_s[s, pl.ds(64, 8), :] = squeeze(t_edges, lane0)
+
+    neighbours = 0
+    for dr, dc in DIRS:
+        neighbours = neighbours + there(dr, dc).astype(jnp.int32)
+    pl.semaphore_wait(barrier, neighbours)
+
+    row_exchange, first_exchange = [], []
+    for s in range(2):
+        row_exchange.append((DIRS[s], ra_s.at[s], ra_r.at[1 - s], s, 1 - s))
+        first_exchange.append((DIRS[s], rb_s.at[s], rb_r.at[1 - s], 2 + s, 3 - s))
+    for s in range(4):
+        first_exchange.append(
+            (DIRS[4 + s], rb_s.at[s // 2, pl.ds(0, 24)], cr_r.at[3 - s], 6 + s, 9 - s)
+        )
+    for s in range(2):
+        first_exchange.append((DIRS[2 + s], cm_s.at[s], cm_r.at[1 - s], 4 + s, 5 - s))
+    second_exchange = []
+    for s in range(2):
+        second_exchange.append((DIRS[s], r2_s.at[s], r2_r.at[1 - s], s, 1 - s))
+        second_exchange.append((DIRS[2 + s], c2_s.at[s], c2_r.at[1 - s], 2 + s, 3 - s))
+    for s in range(4):
+        second_exchange.append(
+            (DIRS[4 + s], k2_s.at[s // 2], k2_r.at[3 - s], 4 + s, 7 - s)
+        )
+
+    def start(exchange, sends, recvs):
+        for (dr, dc), src, dst, a, b in exchange:
+
+            @pl.when(there(dr, dc))
+            def _(dr=dr, dc=dc, src=src, dst=dst, a=a, b=b):
+                remote(src, dst, sends.at[a], recvs.at[b], dr, dc).start()
+
+    def wait_recv(exchange, sends, recvs):
+        for (dr, dc), src, dst, a, b in exchange:
+
+            @pl.when(there(-dr, -dc))
+            def _(dr=dr, dc=dc, src=src, dst=dst, a=a, b=b):
+                remote(src, dst, sends.at[a], recvs.at[b], -dr, -dc).wait_recv()
+
+    def wait_send(exchange, sends, recvs):
+        for (dr, dc), src, dst, a, b in exchange:
+
+            @pl.when(there(dr, dc))
+            def _(dr=dr, dc=dc, src=src, dst=dst, a=a, b=b):
+                remote(src, dst, sends.at[a], recvs.at[b], dr, dc).wait_send()
+
     start(first_exchange, send_sem, recv_sem)
+    start(row_exchange, send_sem, recv_sem)
 
     for ref, _ in nodes:
         ref[:, :, pl.ds(S0 + 4, 8), :] = ref[:, :, pl.ds(M0, 8), :]
@@ -586,11 +602,14 @@
         load[t] = GAIN * mine
 
     l_edges = pack_edges([(load[t], load[t]) for t in range(4)])
-    c2_s[...] = l_edges
-    for s, cell in ((0, 0), (1, 28)):
-        r2_s[s, pl.ds(0, 4), :] = l_edges[cell : cell + 4]
+    for s, (cell, lane0) in enumerate(((0, 20), (28, 8))):
+        c2_s[s] = squeeze(l_edges, lane0)
+        k2_s[s, pl.ds(0, 4), :] = l_edges[cell : cell + 4]
         for t in range(4):
-            r2_s[s, pl.ds(8 + 4 * t, 4), :] = load[t, pl.ds(cell, 4), :]
+            r2_s[s, pl.ds(4 * t, 4), :] = load[t, pl.ds(cell, 4), :]
+        for t in range(3):
+            own, free = (t, 3) if s == 0 else (29 + t, 0)
+            r2_s[s, pl.ds(4 * t + free, 1), :] = l_edges[own : own + 1]
     start(second_exchange, send2_sem, recv2_sem)
 
     x3[:, :, pl.ds(M0, 4), :] = x3[:, :, pl.ds(S0 + 4, 4), :]
@@ -604,10 +623,10 @@
         tt[t, pl.ds(0, 4), :] = rb_r[0, pl.ds(24 + 4 * t, 4), :]
         tt[t, pl.ds(4, 32), :] = t_raw[t]
         tt[t, pl.ds(36, 4), :] = rb_r[1, pl.ds(24 + 4 * t, 4), :]
-    cells = pl.ds(64, 32)
+    cells = pl.ds(64, 8)
     edge = pl.ds(16, 4)
     ht[pl.ds(0, 4), :] = with_sides(rb_r[0, edge, :], cr_r[0, edge, :], cr_r[1, edge, :])
-    ht[pl.ds(4, 32), :] = with_sides(t_edges, cm_r[0, cells, :], cm_r[1, cells, :])
+    ht[pl.ds(4, 32), :] = with_squeezed_sides(t_edges, cm_r[0, cells, :], cm_r[1, cells, :])
     ht[pl.ds(36, 4), :] = with_sides(rb_r[1, edge, :], cr_r[2, edge, :], cr_r[3, edge, :])
     heat_of = Heat(n_row, n_col, ts, tu, hs, hu)
     theta, side = tt[...], ht[...]
@@ -616,13 +635,19 @@
 
     wait_recv(second_exchange, send2_sem, recv2_sem)
     for t in range(4):
-        tl[t, pl.ds(0, 4), :] = r2_r[0, pl.ds(8 + 4 * t, 4), :]
+        tl[t, pl.ds(0, 4), :] = r2_r[0, pl.ds(4 * t, 4), :]
         tl[t, pl.ds(4, 32), :] = load[t]
-        tl[t, pl.ds(36, 4), :] = r2_r[1, pl.ds(8 + 4 * t, 4), :]
-    edge = pl.ds(0, 4)
-    hl[pl.ds(0, 4), :] = with_sides(r2_r[0, edge, :], k2_r[0, edge, :], k2_r[1, edge, :])
-    hl[pl.ds(4, 32), :] = with_sides(l_edges, c2_r[0], c2_r[1])
-    hl[pl.ds(36, 4), :] = with_sides(r2_r[1, edge, :], k2_r[2, edge, :], k2_r[3, edge, :])
+        tl[t, pl.ds(36, 4), :] = r2_r[1, pl.ds(4 * t, 4), :]
+    zero = jnp.zeros((1, 128), F32)
+    above = [zero] + [r2_r[0, pl.ds(4 * t, 1), :] for t in range(3)]
+    below = [r2_r[1, pl.ds(4 * t + 3, 1), :] for t in range(3)] + [zero]
+    for first, corner, rows in ((0, 0, above), (36, 2, below)):
+        hl[pl.ds(first, 4), :] = with_sides(
+            jnp.concatenate(rows, axis=0),
+            k2_r[corner, pl.ds(0, 4), :],
+            k2_r[corner + 1, pl.ds(0, 4), :],
+        )
+    hl[pl.ds(4, 32), :] = with_squeezed_sides(l_edges, c2_r[0], c2_r[1])
 
     wait_send(row_exchange, send_sem, recv_sem)
     wait_send(first_exchange, send_sem, recv_sem)
@@ -733,15 +758,15 @@
         *[vmem(*strip) for _ in range(6)],
         vmem(2, 15, 2, 8, 128), vmem(2, 15, 2, 8, 128),
         vmem(2, 40, 128), vmem(2, 40, 128),
-        vmem(2, 96, 128), vmem(2, 96, 128),
+        vmem(2, 72, 128), vmem(2, 72, 128),
         vmem(4, 24, 128),
         vmem(4, 32, 128),
-        vmem(2, 24, 128), vmem(2, 24, 128),
-        vmem(32, 128), vmem(2, 32, 128),
-        vmem(4, 8, 128),
+        vmem(2, 16, 128), vmem(2, 16, 128),
+        vmem(2, 8, 128), vmem(2, 8, 128),
+        vmem(2, 8, 128), vmem(4, 8, 128),
         *heat,
         vmem(2, 2, 256, 128, dtype=BF16), vmem(256, 128, dtype=BF16),
-        pltpu.SemaphoreType.DMA((16,)),
+        pltpu.SemaphoreType.DMA((1 + 5 * GROUPS,)),
         pltpu.SemaphoreType.DMA((10,)),
         pltpu.SemaphoreType.DMA((10,)),
         pltpu.SemaphoreType.DMA((8,)),

time: 20.7 us -> 20.3 us (0.981)
  Pallas kernels: 19.9 us -> 19.5 us
    pallas_call x1, Pallas kernels: 18.6 us -> 18.2 us  [on_device(): pl.pallas_call(functools.partial(kernel, n_row, n_col), out_shape=tuple((...]
where the time goes in v1:
time: 20.3 us; the launch traced here: 20.2 us
  Pallas kernels  19.5 us (96%)
  between operations  0.64 us (3%)
    pallas_call x1, Pallas kernels, on_device(): pl.pallas_call(functools.partial(kernel, n_row, n_col), out_shape=tuple((...  18.2 us
    pallas_call x1, Pallas kernels, on_device(): pl.pallas_call(functools.partial(finish, n_row, n_col), out_shape=(jax.Sh...  1.33 us

profile of v1, /device:TPU:1, one launch (start us, length us, event | category | flops | bytes accessed | tf_op | source)
XLA Modules:
  0.0 20.2 jit_solution(18173176369224709320)
XLA Ops:
  0.6 18.2 %shard_map.77 = (f32[4,4,176,128]{3,2,1,0:T(8,128)S(1)}, f32[4,40,128]{2,1,0:T(8,128)S(1)}, f32[40,128]{1,0:T(8,128)S(1)}, f32[4,40,128]{2,1,0:T(8,128)S(1)}, f32[40,128]{1,0:T(8,128)S(1)}) custom-call(f32[4,128,512]{2,1,0:T(8,128)} %v_h.1, f32[4,128,512]{2,1,0:T(8,128)} %a_h.1, f32[4,32,128]{2,1,0:T(8,128)} %t_h.1, s32[3,128,512]{2,1,0:T(8,128)} %vi_h.1, ...), custom_call_target="tpu_custom_call" | custom-call | tf_op jit(solution)/shard_map/pallas_call | solution.py:777
  18.8 1.3 %shard_map.78 = (f32[4,128,512]{2,1,0:T(8,128)}, f32[4,32,128]{2,1,0:T(8,128)}) custom-call(f32[4,4,176,128]{3,2,1,0:T(8,128)S(1)} %get-tuple-element.7.x3, f32[4,40,128]{2,1,0:T(8,128)S(1)} %get-tuple-element.8.tt, f32[40,128]{1,0:T(8,128)S(1)} %get-tuple-element.9.ht, f32[4,40,128]{2,1,0:T(8,128)S(1)} %get-tuple-element.10.tl, ...), custom_call_target="tpu_custom_call" | custom-call | tf_op jit(solution)/shard_map/pallas_call | solution.py:792

commit v2 on v1

--- a/solution.py
+++ b/solution.py
@@ -26,6 +26,7 @@
 STRIP_UNROLL = 3
 GROUPS = 4
 GROUP = 32
+ORDER = (0, 3, 1, 2)
 
 ROWS = 128
 M0 = 8
@@ -296,7 +297,7 @@
     x, x1, x2, g, j, v, inv, gr, lr, lg, lw, wa, wb, wc, p0, p1, p2,
     expand, x_raw, a_raw, vi_raw, fe_raw, in_raw, t_raw,
     qx, qx1, qx2, qx3, qg, qj, qv, qi, qgr, qlr, qlg, qlw, qa, qb, qc, q0, q1, q2,
-    ra_s, ra_r, rb_s, rb_r, cm_s, cm_r, cr_r,
+    ra_s, ra_r, rc_s, rc_r, rb_s, rb_r, cm_s, cm_r, cr_r,
     load, r2_s, r2_r, c2_s, c2_r, k2_s, k2_r, ts, tu, hs, hu, pick, pick_ends,
     in_sem, send_sem, recv_sem, send2_sem, recv2_sem,
 ):
@@ -337,7 +338,7 @@
 
     fetch("t", t_h, t_raw)
     inputs = ((a_h, a_raw), (v_h, x_raw), (fe_h, fe_raw), (in_h, in_raw), (vi_h, vi_raw))
-    for n in range(GROUPS):
+    for n in ORDER:
         for src, dst in inputs:
             rows = pl.ds(n * GROUP, GROUP)
             fetch(n, src.at[:, rows, :], dst.at[:, rows, :])
@@ -350,6 +351,9 @@
     for ref in (x3, g, wa, wb, wc):
         for start in (0, M0 + ROWS, S0 + 24):
             ref[:, :, pl.ds(start, 8), :] = jnp.zeros((4, 4, 8, 128), F32)
+    for ref, tiers in ((j, 4), (v, 3)):
+        for start in (0, 16):
+            ref[:, :, pl.ds(S0 + start, 8), :] = jnp.zeros((tiers, 4, 8, 128), F32)
     for ref in (qx, qx3, qg, qj, qv, qa, qb, qc):
         for start in (0, Q0 + ROWS):
             ref[pl.ds(start, 16), :] = jnp.zeros((16, 128), F32)
@@ -361,11 +365,13 @@
             ref[pl.ds(start, 8), :] = jnp.zeros((8, 128), F32)
     for s in range(2):
         rb_s[s, pl.ds(16, 8), :] = jnp.zeros((8, 128), F32)
+        rc_s[s, pl.ds(80, 8), :] = jnp.zeros((8, 128), F32)
         k2_s[s] = jnp.zeros((8, 128), F32)
 
         @pl.when(jnp.logical_not(there(*DIRS[s])))
         def _(s=s):
-            ra_r[s] = jnp.zeros((15, 2, 8, 128), F32)
+            ra_r[s] = jnp.zeros((8, 2, 8, 128), F32)
+            rc_r[s] = jnp.zeros((88, 128), F32)
             rb_r[s] = jnp.zeros((40, 128), F32)
             r2_r[s] = jnp.zeros((16, 128), F32)
 
@@ -433,24 +439,91 @@
 
     nodes = ((x, 4), (g, 4), (j, 4), (v, 3))
     strips = (qx, qg, qj, qv)
-
-    for n in range(GROUPS):
+    three_deep = [
+        (3 * (16 * k + 4 * t + b), ref, t, b)
+        for k, (ref, tiers) in enumerate(((j, 4), (v, 3)))
+        for t in range(tiers)
+        for b in range(4)
+    ]
+
+    row_exchange, first_exchange = [], []
+    for s in range(2):
+        row_exchange.append((DIRS[s], ra_s.at[s], ra_r.at[1 - s], s, 1 - s))
+        row_exchange.append((DIRS[s], rc_s.at[s], rc_r.at[1 - s], 10 + s, 11 - s))
+        first_exchange.append((DIRS[s], rb_s.at[s], rb_r.at[1 - s], 2 + s, 3 - s))
+    for s in range(4):
+        first_exchange.append(
+            (DIRS[4 + s], rb_s.at[s // 2, pl.ds(0, 24)], cr_r.at[3 - s], 6 + s, 9 - s)
+        )
+    for s in range(2):
+        first_exchange.append((DIRS[2 + s], cm_s.at[s], cm_r.at[1 - s], 4 + s, 5 - s))
+    second_exchange = []
+    for s in range(2):
+        second_exchange.append((DIRS[s], r2_s.at[s], r2_r.at[1 - s], s, 1 - s))
+        second_exchange.append((DIRS[2 + s], c2_s.at[s], c2_r.at[1 - s], 2 + s, 3 - s))
+    for s in range(4):
+        second_exchange.append(
+            (DIRS[4 + s], k2_s.at[s // 2], k2_r.at[3 - s], 4 + s, 7 - s)
+        )
+
+    def start(exchange, sends, recvs):
+        for (dr, dc), src, dst, a, b in exchange:
+
+            @pl.when(there(dr, dc))
+            def _(dr=dr, dc=dc, src=src, dst=dst, a=a, b=b):
+                remote(src, dst, sends.at[a], recvs.at[b], dr, dc).start()
+
+    def wait_recv(exchange, sends, recvs):
+        for (dr, dc), src, dst, a, b in exchange:
+
+            @pl.when(there(-dr, -dc))
+            def _(dr=dr, dc=dc, src=src, dst=dst, a=a, b=b):
+                remote(src, dst, sends.at[a], recvs.at[b], -dr, -dc).wait_recv()
+
+    def wait_send(exchange, sends, recvs):
+        for (dr, dc), src, dst, a, b in exchange:
+
+            @pl.when(there(dr, dc))
+            def _(dr=dr, dc=dc, src=src, dst=dst, a=a, b=b):
+                remote(src, dst, sends.at[a], recvs.at[b], dr, dc).wait_send()
+
+    def ready(n):
         arrived(n)
         for off in range(n * GROUP, (n + 1) * GROUP, 8):
             prepare(off)
+
+    def pack(n):
         tile = pl.ds(M0 + n * GROUP, GROUP)
         for (ref, tiers), packed in zip(nodes, strips):
             packed[pl.ds(Q0 + n * GROUP, GROUP), :] = pack_edges(
                 [(ref[t, 0, tile, :], ref[t, 3, tile, :]) for t in range(tiers)]
             )
-    tile = pl.ds(M0, ROWS)
-
+
+    for n in ORDER[:2]:
+        ready(n)
     for s, first in ((0, 0), (1, ROWS - 4)):
-        for k, (ref, tiers) in enumerate(nodes):
+        for k, ref in enumerate((x, g)):
             for h in range(2):
-                ra_s[s, pl.ds(4 * k, tiers), :, pl.ds(4 * h, 4), :] = ref[
+                ra_s[s, pl.ds(4 * k, 4), :, pl.ds(4 * h, 4), :] = ref[
                     :, pl.ds(2 * h, 2), pl.ds(M0 + first, 4), :
                 ]
+        first = (0, ROWS - 3)[s]
+        for at, ref, t, b in three_deep:
+            rc_s[s, pl.ds(at, 3), :] = ref[t, b, pl.ds(M0 + first, 3), :]
+
+    neighbours = 0
+    for dr, dc in DIRS:
+        neighbours = neighbours + there(dr, dc).astype(jnp.int32)
+    pl.semaphore_wait(barrier, neighbours)
+    start(row_exchange, send_sem, recv_sem)
+
+    for n in ORDER[:2]:
+        pack(n)
+    for n in ORDER[2:]:
+        ready(n)
+        pack(n)
+    tile = pl.ds(M0, ROWS)
+
     t_edges = pack_edges([(t_raw[t], t_raw[t]) for t in range(4)])
     for s, first in ((0, 0), (1, ROWS - 4)):
         for k, packed in enumerate(strips):
@@ -471,54 +544,7 @@
                 mixed = jnp.where(group == slot32 // 4, part, mixed)
         cm_s[s, pl.ds(0, 64), :] = mixed
         cm_s[s, pl.ds(64, 8), :] = squeeze(t_edges, lane0)
-
-    neighbours = 0
-    for dr, dc in DIRS:
-        neighbours = neighbours + there(dr, dc).astype(jnp.int32)
-    pl.semaphore_wait(barrier, neighbours)
-
-    row_exchange, first_exchange = [], []
-    for s in range(2):
-        row_exchange.append((DIRS[s], ra_s.at[s], ra_r.at[1 - s], s, 1 - s))
-        first_exchange.append((DIRS[s], rb_s.at[s], rb_r.at[1 - s], 2 + s, 3 - s))
-    for s in range(4):
-        first_exchange.append(
-            (DIRS[4 + s], rb_s.at[s // 2, pl.ds(0, 24)], cr_r.at[3 - s], 6 + s, 9 - s)
-        )
-    for s in range(2):
-        first_exchange.append((DIRS[2 + s], cm_s.at[s], cm_r.at[1 - s], 4 + s, 5 - s))
-    second_exchange = []
-    for s in range(2):
-        second_exchange.append((DIRS[s], r2_s.at[s], r2_r.at[1 - s], s, 1 - s))
-        second_exchange.append((DIRS[2 + s], c2_s.at[s], c2_r.at[1 - s], 2 + s, 3 - s))
-    for s in range(4):
-        second_exchange.append(
-            (DIRS[4 + s], k2_s.at[s // 2], k2_r.at[3 - s], 4 + s, 7 - s)
-        )
-
-    def start(exchange, sends, recvs):
-        for (dr, dc), src, dst, a, b in exchange:
-
-            @pl.when(there(dr, dc))
-            def _(dr=dr, dc=dc, src=src, dst=dst, a=a, b=b):
-                remote(src, dst, sends.at[a], recvs.at[b], dr, dc).start()
-
-    def wait_recv(exchange, sends, recvs):
-        for (dr, dc), src, dst, a, b in exchange:
-
-            @pl.when(there(-dr, -dc))
-            def _(dr=dr, dc=dc, src=src, dst=dst, a=a, b=b):
-                remote(src, dst, sends.at[a], recvs.at[b], -dr, -dc).wait_recv()
-
-    def wait_send(exchange, sends, recvs):
-        for (dr, dc), src, dst, a, b in exchange:
-
-            @pl.when(there(dr, dc))
-            def _(dr=dr, dc=dc, src=src, dst=dst, a=a, b=b):
-                remote(src, dst, sends.at[a], recvs.at[b], dr, dc).wait_send()
-
     start(first_exchange, send_sem, recv_sem)
-    start(row_exchange, send_sem, recv_sem)
 
     for ref, _ in nodes:
         ref[:, :, pl.ds(S0 + 4, 8), :] = ref[:, :, pl.ds(M0, 8), :]
@@ -537,11 +563,14 @@
     wait_recv(first_exchange, send_sem, recv_sem)
 
     for s, first in ((0, 0), (1, 20)):
-        for k, (ref, tiers) in enumerate(nodes):
+        for k, ref in enumerate((x, g)):
             for h in range(2):
                 ref[:, pl.ds(2 * h, 2), pl.ds(S0 + first, 4), :] = ra_r[
-                    s, pl.ds(4 * k, tiers), :, pl.ds(4 * h, 4), :
+                    s, pl.ds(4 * k, 4), :, pl.ds(4 * h, 4), :
                 ]
+        first = (1, 20)[s]
+        for at, ref, t, b in three_deep:
+            ref[t, b, pl.ds(S0 + first, 3), :] = rc_r[s, pl.ds(at, 3), :]
     strip = pl.ds(S0, 24)
     wa[:, :, strip, :] = g[:, :, strip, :] * x[:, :, strip, :]
 
@@ -756,7 +785,8 @@
         *[vmem(*strip) for _ in range(9)],
         *[vmem(STRIP_UNROLL, 48, 128) for _ in range(3)],
         *[vmem(*strip) for _ in range(6)],
-        vmem(2, 15, 2, 8, 128), vmem(2, 15, 2, 8, 128),
+        vmem(2, 8, 2, 8, 128), vmem(2, 8, 2, 8, 128),
+        vmem(2, 88, 128), vmem(2, 88, 128),
         vmem(2, 40, 128), vmem(2, 40, 128),
         vmem(2, 72, 128), vmem(2, 72, 128),
         vmem(4, 24, 128),
@@ -767,8 +797,8 @@
         *heat,
         vmem(2, 2, 256, 128, dtype=BF16), vmem(256, 128, dtype=BF16),
         pltpu.SemaphoreType.DMA((1 + 5 * GROUPS,)),
-        pltpu.SemaphoreType.DMA((10,)),
-        pltpu.SemaphoreType.DMA((10,)),
+        pltpu.SemaphoreType.DMA((12,)),
+        pltpu.SemaphoreType.DMA((12,)),
         pltpu.SemaphoreType.DMA((8,)),
         pltpu.SemaphoreType.DMA((8,)),
     ]

time: 20.3 us -> 19.6 us (0.966)
  Pallas kernels: 19.5 us -> 18.8 us
    pallas_call x1, Pallas kernels: 18.2 us -> 17.5 us  [on_device(): pl.pallas_call(functools.partial(kernel, n_row, n_col), out_shape=tuple((...]
where the time goes in v2:
time: 19.6 us; the launch traced here: 19.5 us
  Pallas kernels  18.8 us (96%)
  between operations  0.64 us (3%)
    pallas_call x1, Pallas kernels, on_device(): pl.pallas_call(functools.partial(kernel, n_row, n_col), out_shape=tuple((...  17.5 us
    pallas_call x1, Pallas kernels, on_device(): pl.pallas_call(functools.partial(finish, n_row, n_col), out_shape=(jax.Sh...  1.33 us

profile of v2, /device:TPU:1, one launch (start us, length us, event | category | flops | bytes accessed | tf_op | source)
XLA Modules:
  0.0 19.5 jit_solution(6673966590722888817)
XLA Ops:
  0.6 17.5 %shard_map.77 = (f32[4,4,176,128]{3,2,1,0:T(8,128)S(1)}, f32[4,40,128]{2,1,0:T(8,128)S(1)}, f32[40,128]{1,0:T(8,128)S(1)}, f32[4,40,128]{2,1,0:T(8,128)S(1)}, f32[40,128]{1,0:T(8,128)S(1)}) custom-call(f32[4,128,512]{2,1,0:T(8,128)} %v_h.1, f32[4,128,512]{2,1,0:T(8,128)} %a_h.1, f32[4,32,128]{2,1,0:T(8,128)} %t_h.1, s32[3,128,512]{2,1,0:T(8,128)} %vi_h.1, ...), custom_call_target="tpu_custom_call" | custom-call | tf_op jit(solution)/shard_map/pallas_call | solution.py:807
  18.1 1.3 %shard_map.78 = (f32[4,128,512]{2,1,0:T(8,128)}, f32[4,32,128]{2,1,0:T(8,128)}) custom-call(f32[4,4,176,128]{3,2,1,0:T(8,128)S(1)} %get-tuple-element.7.x3, f32[4,40,128]{2,1,0:T(8,128)S(1)} %get-tuple-element.8.tt, f32[40,128]{1,0:T(8,128)S(1)} %get-tuple-element.9.ht, f32[4,40,128]{2,1,0:T(8,128)S(1)} %get-tuple-element.10.tl, ...), custom_call_target="tpu_custom_call" | custom-call | tf_op jit(solution)/shard_map/pallas_call | solution.py:822

commit v3 on v2

--- a/solution.py
+++ b/solution.py
@@ -24,9 +24,7 @@
 GAIN = 0.0625
 MAIN_UNROLL = 4
 STRIP_UNROLL = 3
-GROUPS = 4
-GROUP = 32
-ORDER = (0, 3, 1, 2)
+GROUPS = ((0, 8), (120, 8), (8, 56), (64, 56))
 
 ROWS = 128
 M0 = 8
@@ -338,10 +336,10 @@
 
     fetch("t", t_h, t_raw)
     inputs = ((a_h, a_raw), (v_h, x_raw), (fe_h, fe_raw), (in_h, in_raw), (vi_h, vi_raw))
-    for n in ORDER:
+    for first, size in GROUPS:
         for src, dst in inputs:
-            rows = pl.ds(n * GROUP, GROUP)
-            fetch(n, src.at[:, rows, :], dst.at[:, rows, :])
+            rows = pl.ds(first, size)
+            fetch(first, src.at[:, rows, :], dst.at[:, rows, :])
 
     def arrived(*names):
         for name in names:
@@ -487,20 +485,20 @@
             def _(dr=dr, dc=dc, src=src, dst=dst, a=a, b=b):
                 remote(src, dst, sends.at[a], recvs.at[b], dr, dc).wait_send()
 
-    def ready(n):
-        arrived(n)
-        for off in range(n * GROUP, (n + 1) * GROUP, 8):
+    def ready(first, size):
+        arrived(first)
+        for off in range(first, first + size, 8):
             prepare(off)
 
-    def pack(n):
-        tile = pl.ds(M0 + n * GROUP, GROUP)
+    def pack(first, size):
+        tile = pl.ds(M0 + first, size)
         for (ref, tiers), packed in zip(nodes, strips):
-            packed[pl.ds(Q0 + n * GROUP, GROUP), :] = pack_edges(
+            packed[pl.ds(Q0 + first, size), :] = pack_edges(
                 [(ref[t, 0, tile, :], ref[t, 3, tile, :]) for t in range(tiers)]
             )
 
-    for n in ORDER[:2]:
-        ready(n)
+    for group in GROUPS[:2]:
+        ready(*group)
     for s, first in ((0, 0), (1, ROWS - 4)):
         for k, ref in enumerate((x, g)):
             for h in range(2):
@@ -517,11 +515,11 @@
     pl.semaphore_wait(barrier, neighbours)
     start(row_exchange, send_sem, recv_sem)
 
-    for n in ORDER[:2]:
-        pack(n)
-    for n in ORDER[2:]:
-        ready(n)
-        pack(n)
+    for group in GROUPS[:2]:
+        pack(*group)
+    for group in GROUPS[2:]:
+        ready(*group)
+        pack(*group)
     tile = pl.ds(M0, ROWS)
 
     t_edges = pack_edges([(t_raw[t], t_raw[t]) for t in range(4)])
@@ -559,6 +557,32 @@
     )
     solve(range(4), ROWS // 8, MAIN_UNROLL, (big, M0, 8))
 
+    def cell_rows(parts, first, cells):
+        take = lambda ref, k: ref[
+            (slice(None),) * (len(ref.shape) - 2)
+            + (pl.ds(first + k, cells, 4), slice(None))
+        ]
+        total = 0.5 * (take(parts[2], -1) - take(parts[2], 3))
+        right = take(parts[1], 0)
+        for k in range(4):
+            total = total + take(parts[0], k)
+            if k:
+                right = right + take(parts[1], k)
+        return total, right
+
+    def tile_cells(first, cells):
+        total = jnp.zeros((4 * cells, 128), F32)
+        for k, values in enumerate(cell_rows(big.power, first, cells)):
+            blocks = [values[:, b].reshape(4 * cells, 128) for b in range(4)]
+            for h in range(2):
+                both = jnp.concatenate(blocks[2 * h : 2 * h + 2], axis=1)
+                total = total + dot3(both, pick[h, k])
+        return GAIN * total
+
+    inner_cells = tile_cells(M0, 32)
+    for t in range(4):
+        load[t] = inner_cells[32 * t : 32 * (t + 1)]
+
     wait_recv(row_exchange, send_sem, recv_sem)
     wait_recv(first_exchange, send_sem, recv_sem)
 
@@ -595,40 +619,19 @@
     qa[strip, :] = qg[strip, :] * qx[strip, :]
     solve(range(4), 3, STRIP_UNROLL, (big, S0, 8), (side, 8, 48))
 
-    for ref, before in ((p0, 0), (p1, 0), (p2, 1)):
-        ref[:, :, pl.ds(M0 - before, 4 + before), :] = ref[
-            :, :, pl.ds(S0 + 4 - before, 4 + before), :
-        ]
-        ref[:, :, pl.ds(M0 + ROWS - 4, 4), :] = ref[:, :, pl.ds(S0 + 16, 4), :]
-
-    def cell_rows(parts, first):
-        take = lambda ref, k: ref[
-            (slice(None),) * (len(ref.shape) - 2) + (pl.ds(first + k, 32, 4), slice(None))
-        ]
-        total = 0.5 * (take(parts[2], -1) - take(parts[2], 3))
-        right = take(parts[1], 0)
-        for k in range(4):
-            total = total + take(parts[0], k)
-            if k:
-                right = right + take(parts[1], k)
-        return total, right
-
-    sums, rights = cell_rows(big.power, M0)
-    edge_sums, edge_rights = cell_rows(side.power, Q0)
-    total = jnp.zeros((128, 128), F32)
-    for h in range(2):
-        for k, values in enumerate((sums, rights)):
-            both = jnp.concatenate(
-                [values[:, 2 * h].reshape(128, 128), values[:, 2 * h + 1].reshape(128, 128)],
-                axis=1,
-            )
-            total = total + dot3(both, pick[h, k])
-    ends = dot3(jnp.concatenate([edge_sums, edge_rights], axis=1), pick_ends[...])
+    for t, (first, last) in enumerate(
+        (rows[8 * t : 8 * t + 1], rows[8 * t + 3 : 8 * t + 4])
+        for rows in [tile_cells(S0 + 4, 8)]
+        for t in range(4)
+    ):
+        load[t, pl.ds(0, 1), :] = first
+        load[t, pl.ds(31, 1), :] = last
+    values = cell_rows(side.power, Q0, 32)
+    ends = GAIN * dot3(jnp.concatenate(values, axis=1), pick_ends[...])
     lane = iota((32, 128), 1)
     for t in range(4):
         mine = pltpu.roll(ends, (-32 * t) % 128, 1) if t else ends
-        mine = jnp.where((lane == 0) | (lane == 127), mine, total[32 * t : 32 * (t + 1)])
-        load[t] = GAIN * mine
+        load[t] = jnp.where((lane == 0) | (lane == 127), mine, load[t])
 
     l_edges = pack_edges([(load[t], load[t]) for t in range(4)])
     for s, (cell, lane0) in enumerate(((0, 20), (28, 8))):
@@ -699,13 +702,12 @@
 
     @staticmethod
     def flux(theta, s, u, s_ref, u_ref, rows, axis):
-        def near(ref, mid):
-            around = ref[rows(7)] + ref[rows(9)]
-            return around + pltpu.roll(mid, 1, axis) + pltpu.roll(mid, 127, axis)
-
         s_ref[rows(8)] = s
         u_ref[rows(8)] = u
-        return s * (near(u_ref, u) - theta * near(s_ref, s))
+        near = lambda ref: ref[rows(7)] + ref[rows(9)]
+        right = lambda x: pltpu.roll(x, 127, axis)
+        e = s * right(s) * (right(theta) - theta)
+        return s * (near(u_ref) - theta * near(s_ref)) + (e - pltpu.roll(e, 1, axis))
 
     def tile(self, theta):
         s = jnp.exp(-0.15 * theta) * self.row_mask
@@ -779,7 +781,8 @@
         *[vmem(*node) for _ in range(5)], vmem(3, *node[1:]),
         *[vmem(*node) for _ in range(2)],
         *[vmem(MAIN_UNROLL, 4, 4, 8, 128) for _ in range(3)],
-        *[vmem(*node) for _ in range(6)],
+        *[vmem(*node) for _ in range(3)],
+        *[vmem(4, 4, R_ALL + 8, 128) for _ in range(3)],
         vmem(4, 4, ROWS, 128), vmem(*raw), vmem(*raw), vmem(3, *raw[1:], dtype=jnp.int32),
         vmem(*raw, dtype=jnp.int32), vmem(*raw), vmem(4, 32, 128),
         *[vmem(*strip) for _ in range(9)],
@@ -796,7 +799,7 @@
         vmem(2, 8, 128), vmem(4, 8, 128),
         *heat,
         vmem(2, 2, 256, 128, dtype=BF16), vmem(256, 128, dtype=BF16),
-        pltpu.SemaphoreType.DMA((1 + 5 * GROUPS,)),
+        pltpu.SemaphoreType.DMA((1 + 5 * len(GROUPS),)),
         pltpu.SemaphoreType.DMA((12,)),
         pltpu.SemaphoreType.DMA((12,)),
         pltpu.SemaphoreType.DMA((8,)),

time: 19.6 us -> 19.6 us (level)
  no operation moved by 1% of the time
where the time goes in v3:
time: 19.6 us; the launch traced here: 19.5 us
  Pallas kernels  18.9 us (96%)
  between operations  0.64 us (3%)
    pallas_call x1, Pallas kernels, on_device(): pl.pallas_call(functools.partial(kernel, n_row, n_col), out_shape=tuple((...  17.5 us
    pallas_call x1, Pallas kernels, on_device(): pl.pallas_call(functools.partial(finish, n_row, n_col), out_shape=(jax.Sh...  1.41 us

profile of v3, /device:TPU:1, one launch (start us, length us, event | category | flops | bytes accessed | tf_op | source)
XLA Modules:
  0.0 19.5 jit_solution(17693554898644036409)
XLA Ops:
  0.6 17.5 %shard_map.77 = (f32[4,4,176,128]{3,2,1,0:T(8,128)S(1)}, f32[4,40,128]{2,1,0:T(8,128)S(1)}, f32[40,128]{1,0:T(8,128)S(1)}, f32[4,40,128]{2,1,0:T(8,128)S(1)}, f32[40,128]{1,0:T(8,128)S(1)}) custom-call(f32[4,128,512]{2,1,0:T(8,128)} %v_h.1, f32[4,128,512]{2,1,0:T(8,128)} %a_h.1, f32[4,32,128]{2,1,0:T(8,128)} %t_h.1, s32[3,128,512]{2,1,0:T(8,128)} %vi_h.1, ...), custom_call_target="tpu_custom_call" | custom-call | tf_op jit(solution)/shard_map/pallas_call | solution.py:810
  18.1 1.4 %shard_map.78 = (f32[4,128,512]{2,1,0:T(8,128)}, f32[4,32,128]{2,1,0:T(8,128)}) custom-call(f32[4,4,176,128]{3,2,1,0:T(8,128)S(1)} %get-tuple-element.7.x3, f32[4,40,128]{2,1,0:T(8,128)S(1)} %get-tuple-element.8.tt, f32[40,128]{1,0:T(8,128)S(1)} %get-tuple-element.9.ht, f32[4,40,128]{2,1,0:T(8,128)S(1)} %get-tuple-element.10.tl, ...), custom_call_target="tpu_custom_call" | custom-call | tf_op jit(solution)/shard_map/pallas_call | solution.py:825

commit v4 on v3

--- a/solution.py
+++ b/solution.py
@@ -444,17 +444,17 @@
         for b in range(4)
     ]
 
-    row_exchange, first_exchange = [], []
+    row_exchange, col_exchange = [], []
     for s in range(2):
         row_exchange.append((DIRS[s], ra_s.at[s], ra_r.at[1 - s], s, 1 - s))
         row_exchange.append((DIRS[s], rc_s.at[s], rc_r.at[1 - s], 10 + s, 11 - s))
-        first_exchange.append((DIRS[s], rb_s.at[s], rb_r.at[1 - s], 2 + s, 3 - s))
+        row_exchange.append((DIRS[s], rb_s.at[s], rb_r.at[1 - s], 2 + s, 3 - s))
     for s in range(4):
-        first_exchange.append(
+        row_exchange.append(
             (DIRS[4 + s], rb_s.at[s // 2, pl.ds(0, 24)], cr_r.at[3 - s], 6 + s, 9 - s)
         )
     for s in range(2):
-        first_exchange.append((DIRS[2 + s], cm_s.at[s], cm_r.at[1 - s], 4 + s, 5 - s))
+        col_exchange.append((DIRS[2 + s], cm_s.at[s], cm_r.at[1 - s], 4 + s, 5 - s))
     second_exchange = []
     for s in range(2):
         second_exchange.append((DIRS[s], r2_s.at[s], r2_r.at[1 - s], s, 1 - s))
@@ -509,19 +509,8 @@
         for at, ref, t, b in three_deep:
             rc_s[s, pl.ds(at, 3), :] = ref[t, b, pl.ds(M0 + first, 3), :]
 
-    neighbours = 0
-    for dr, dc in DIRS:
-        neighbours = neighbours + there(dr, dc).astype(jnp.int32)
-    pl.semaphore_wait(barrier, neighbours)
-    start(row_exchange, send_sem, recv_sem)
-
     for group in GROUPS[:2]:
         pack(*group)
-    for group in GROUPS[2:]:
-        ready(*group)
-        pack(*group)
-    tile = pl.ds(M0, ROWS)
-
     t_edges = pack_edges([(t_raw[t], t_raw[t]) for t in range(4)])
     for s, first in ((0, 0), (1, ROWS - 4)):
         for k, packed in enumerate(strips):
@@ -530,6 +519,18 @@
         rb_s[s, pl.ds(16, 4), :] = t_edges[cell : cell + 4]
         for t in range(4):
             rb_s[s, pl.ds(24 + 4 * t, 4), :] = t_raw[t, pl.ds(cell, 4), :]
+
+    neighbours = 0
+    for dr, dc in DIRS:
+        neighbours = neighbours + there(dr, dc).astype(jnp.int32)
+    pl.semaphore_wait(barrier, neighbours)
+    start(row_exchange, send_sem, recv_sem)
+
+    for group in GROUPS[2:]:
+        ready(*group)
+        pack(*group)
+    tile = pl.ds(M0, ROWS)
+
     group = lane32((64, 128)) // 4
     for s, lane0 in ((0, 20), (1, 8)):
         mixed = jnp.zeros((64, 128), F32)
@@ -542,7 +543,7 @@
                 mixed = jnp.where(group == slot32 // 4, part, mixed)
         cm_s[s, pl.ds(0, 64), :] = mixed
         cm_s[s, pl.ds(64, 8), :] = squeeze(t_edges, lane0)
-    start(first_exchange, send_sem, recv_sem)
+    start(col_exchange, send_sem, recv_sem)
 
     for ref, _ in nodes:
         ref[:, :, pl.ds(S0 + 4, 8), :] = ref[:, :, pl.ds(M0, 8), :]
@@ -584,7 +585,7 @@
         load[t] = inner_cells[32 * t : 32 * (t + 1)]
 
     wait_recv(row_exchange, send_sem, recv_sem)
-    wait_recv(first_exchange, send_sem, recv_sem)
+    wait_recv(col_exchange, send_sem, recv_sem)
 
     for s, first in ((0, 0), (1, 20)):
         for k, ref in enumerate((x, g)):
@@ -682,7 +683,7 @@
     hl[pl.ds(4, 32), :] = with_squeezed_sides(l_edges, c2_r[0], c2_r[1])
 
     wait_send(row_exchange, send_sem, recv_sem)
-    wait_send(first_exchange, send_sem, recv_sem)
+    wait_send(col_exchange, send_sem, recv_sem)
     wait_send(second_exchange, send2_sem, recv2_sem)
 
 

time: 19.6 us -> 19.4 us (0.990)
  Pallas kernels: 18.9 us -> 18.6 us
    pallas_call x1, Pallas kernels: 17.5 us -> 17.2 us  [on_device(): pl.pallas_call(functools.partial(kernel, n_row, n_col), out_shape=tuple((...]
where the time goes in v4:
time: 19.4 us; the launch traced here: 19.2 us
  Pallas kernels  18.6 us (96%)
  between operations  0.64 us (3%)
    pallas_call x1, Pallas kernels, on_device(): pl.pallas_call(functools.partial(kernel, n_row, n_col), out_shape=tuple((...  17.2 us
    pallas_call x1, Pallas kernels, on_device(): pl.pallas_call(functools.partial(finish, n_row, n_col), out_shape=(jax.Sh...  1.41 us

profile of v4, /device:TPU:1, one launch (start us, length us, event | category | flops | bytes accessed | tf_op | source)
XLA Modules:
  0.0 19.2 jit_solution(11001614476821746527)
XLA Ops:
  0.6 17.2 %shard_map.77 = (f32[4,4,176,128]{3,2,1,0:T(8,128)S(1)}, f32[4,40,128]{2,1,0:T(8,128)S(1)}, f32[40,128]{1,0:T(8,128)S(1)}, f32[4,40,128]{2,1,0:T(8,128)S(1)}, f32[40,128]{1,0:T(8,128)S(1)}) custom-call(f32[4,128,512]{2,1,0:T(8,128)} %v_h.1, f32[4,128,512]{2,1,0:T(8,128)} %a_h.1, f32[4,32,128]{2,1,0:T(8,128)} %t_h.1, s32[3,128,512]{2,1,0:T(8,128)} %vi_h.1, ...), custom_call_target="tpu_custom_call" | custom-call | tf_op jit(solution)/shard_map/pallas_call | solution.py:811
  17.8 1.4 %shard_map.78 = (f32[4,128,512]{2,1,0:T(8,128)}, f32[4,32,128]{2,1,0:T(8,128)}) custom-call(f32[4,4,176,128]{3,2,1,0:T(8,128)S(1)} %get-tuple-element.7.x3, f32[4,40,128]{2,1,0:T(8,128)S(1)} %get-tuple-element.8.tt, f32[40,128]{1,0:T(8,128)S(1)} %get-tuple-element.9.ht, f32[4,40,128]{2,1,0:T(8,128)S(1)} %get-tuple-element.10.tl, ...), custom_call_target="tpu_custom_call" | custom-call | tf_op jit(solution)/shard_map/pallas_call | solution.py:826
